TPU v7x, 512 devices: a whole 4x4x16 slice. The times are simulated.
512 devices in a mesh: dp: 16 (over z), expert: 32 (over x, y, core).
Axes of the slice: x: 4, y: 4, z: 16, core: 2. Of those that a mesh axis runs over, the one named last changes fastest.
Arguments:
- tokens: bfloat16 [4096, 4096], P('expert', 'dp'), may hold values from -6 to 6
- route_ids: int32 [4096, 8], P('expert'), may hold values from 0 to 31, all different within a row; in each aligned block of 128 rows (0 to 127, 128 to 255, ...) at most 40 rows name the same one
- route_weights: bfloat16 [4096, 8], P('expert'), may hold values from 0.099609375 to 0.3984375
- gate_weight: bfloat16 [32, 4096, 768], P('expert', 'dp'), may hold values from -0.09375 to 0.09375
- up_weight: bfloat16 [32, 4096, 768], P('expert', 'dp'), may hold values from -0.09375 to 0.09375
- down_weight: bfloat16 [32, 768, 4096], P('expert', None, 'dp'), may hold values from -0.21875 to 0.21875
- out_grad: bfloat16 [4096, 4096], P('expert', 'dp'), may hold values from -3 to 3
Outputs:
- mixed: bfloat16 [4096, 4096], P('expert', 'dp')
- input_grad: bfloat16 [4096, 4096], P('expert', 'dp')
- gate_weight_grad: float32 [32, 4096, 768], P('expert', 'dp')
- up_weight_grad: float32 [32, 4096, 768], P('expert', 'dp')
- down_weight_grad: float32 [32, 768, 4096], P('expert', None, 'dp')
Inputs may be any that keep to these rules, and one draw needn't show every extreme that they name: `route_ids`: each row names 8 different experts. In each aligned block of 128 rows (the tokens of one index of expert) no expert is named by more than 40 rows, a bound that some block reaches.
All inputs are finite; a program needn't handle non-finite values.
Results may differ from a plain program's by a relative error of at most 0.039.
Values may be sent and summed in bfloat16 or wider, within the bound.
A program may use at most 64 MiB of HBM per device.

v0:
```python
import jax
import jax.numpy as jnp
from jax import lax
from jax.sharding import PartitionSpec as P


def contract_rows(first_op, second_op):
    return lax.dot_general(
        first_op, second_op, (((0,), (0,)), ((), ())), preferred_element_type=jnp.float32
    )


def contract_cols(first_op, second_op):
    return lax.dot_general(
        first_op, second_op, (((1,), (1,)), ((), ())), preferred_element_type=jnp.float32
    )


def expert_forward(expert_rows, weight_g, weight_u, weight_d):
    partial_gate = jnp.dot(expert_rows, weight_g, preferred_element_type=jnp.float32)
    partial_up = jnp.dot(expert_rows, weight_u, preferred_element_type=jnp.float32)
    gate_pre, up_pre = (
        lax.psum(partial_gate.astype(jnp.bfloat16), "dp").astype(jnp.float32),
        lax.psum(partial_up.astype(jnp.bfloat16), "dp").astype(jnp.float32),
    )
    hidden = (jax.nn.silu(gate_pre) * up_pre).astype(jnp.bfloat16)
    produced = jnp.dot(hidden, weight_d, preferred_element_type=jnp.float32).astype(jnp.bfloat16)
    return (gate_pre, up_pre, hidden, produced)


def expert_backward(expert_rows, upstream, gate_pre, up_pre, hidden, weight_g, weight_u, weight_d):
    partial_value = contract_cols(upstream, weight_d)
    hidden_grad = lax.psum(partial_value.astype(jnp.bfloat16), "dp").astype(jnp.float32)
    sigmoid_gate = jax.nn.sigmoid(gate_pre)
    gate_delta = (
        hidden_grad * up_pre * sigmoid_gate * (1.0 + gate_pre * (1.0 - sigmoid_gate))
    ).astype(jnp.bfloat16)
    up_delta = (hidden_grad * jax.nn.silu(gate_pre)).astype(jnp.bfloat16)
    down_grad = contract_rows(hidden, upstream)
    gate_grad = contract_rows(expert_rows, gate_delta)
    up_grad = contract_rows(expert_rows, up_delta)
    back_rows = (contract_cols(gate_delta, weight_g) + contract_cols(up_delta, weight_u)).astype(
        jnp.bfloat16
    )
    return (gate_grad, up_grad, down_grad, back_rows)


def shards(tokens, route_ids, route_weights, gate_weight, up_weight, down_weight, out_grad):
    expert_count = lax.axis_size("expert")
    tok_count = tokens.shape[0]
    width = tokens.shape[1]
    top_count = route_ids.shape[1]
    capacity = min(tok_count, tok_count * top_count // expert_count + tok_count // 16)
    row_total = expert_count * capacity
    weight_g = gate_weight[0]
    weight_u = up_weight[0]
    weight_d = down_weight[0]
    every_tok, every_grad, every_weight = (
        lax.all_gather(tokens, "expert", axis=0, tiled=True),
        lax.all_gather(out_grad, "expert", axis=0, tiled=True),
        lax.all_gather(route_weights, "expert", axis=0, tiled=True),
    )
    every_ids = lax.all_gather(route_ids, "expert", axis=0, tiled=True)
    my_expert = lax.axis_index("expert")
    chosen = every_ids == my_expert
    hit_count = jnp.sum(chosen.astype(jnp.int32), axis=1).reshape(expert_count, tok_count)
    hit_rank = jnp.cumsum(hit_count, axis=1) - hit_count
    block_start = (jnp.arange(expert_count, dtype=jnp.int32) * capacity)[:, None]
    dest_row = jnp.where(hit_count > 0, block_start + hit_rank, row_total).reshape(-1)
    tok_weight = jnp.sum(jnp.where(chosen, every_weight.astype(jnp.float32), 0.0), axis=1)
    expert_rows = (
        jnp.zeros((row_total, width), jnp.bfloat16).at[dest_row].set(every_tok, mode="drop")
    )
    row_weight = jnp.zeros((row_total,), jnp.float32).at[dest_row].set(tok_weight, mode="drop")
    gate_pre, up_pre, hidden, produced = expert_forward(expert_rows, weight_g, weight_u, weight_d)
    safe_row = jnp.minimum(dest_row, row_total - 1)
    present = (hit_count.reshape(-1) > 0).astype(jnp.float32)[:, None]
    weighted = (
        (row_weight[:, None] * produced.astype(jnp.float32))
        .astype(jnp.bfloat16)
        .astype(jnp.float32)
    )
    mixed = lax.psum_scatter(
        (weighted[safe_row] * present).astype(jnp.bfloat16),
        "expert",
        scatter_dimension=0,
        tiled=True,
    )
    grad_rows = (
        jnp.zeros((row_total, width), jnp.bfloat16).at[dest_row].set(every_grad, mode="drop")
    )
    upstream = (row_weight[:, None] * grad_rows.astype(jnp.float32)).astype(jnp.bfloat16)
    gate_grad, up_grad, down_grad, back_rows = expert_backward(
        expert_rows, upstream, gate_pre, up_pre, hidden, weight_g, weight_u, weight_d
    )
    input_grad = lax.psum_scatter(
        (back_rows.astype(jnp.float32)[safe_row] * present).astype(jnp.bfloat16),
        "expert",
        scatter_dimension=0,
        tiled=True,
    )
    return (mixed, input_grad, gate_grad[None], up_grad[None], down_grad[None])


def solution(mesh):
    return jax.shard_map(
        shards,
        mesh=mesh,
        in_specs=(
            P("expert", "dp"),
            P("expert", None),
            P("expert", None),
            P("expert", "dp", None),
            P("expert", "dp", None),
            P("expert", None, "dp"),
            P("expert", "dp"),
        ),
        out_specs=(
            P("expert", "dp"),
            P("expert", "dp"),
            P("expert", "dp", None),
            P("expert", "dp", None),
            P("expert", None, "dp"),
        ),
        check_vma=False,
    )
```

profile of v0, /device:TPU:2, one launch (start us, length us, event | category | flops | bytes accessed | tf_op | source)
XLA Modules:
  0.0 580.4 jit_solution(8875477676704722195)
XLA Ops:
  7.2 0.7 all-gather.3.cloned.1.call-update
  8.0 0.7 all-gather.5.cloned.1.call-update
  8.7 27.1 %all_gather.13 = bf16[4096,8]{0,1:T(8,128)(2,1)S(1)} all-gather(bf16[128,8]{0,1:T(8,128)(2,1)} %param.9), channel_id=1, replica_groups=mesh['dp'=16,'expert'=32] {'expert'}, dimensions={0}, use_global_device_ids=true | all-gather | bytes 67584 | tf_op jit(solution)/shard_map/all_gather | solution.py:61
  35.8 22.3 %all_gather.12 = s32[4096,8]{0,1:T(8,128)S(1)} all-gather(s32[128,8]{0,1:T(8,128)} %param.8), channel_id=1, replica_groups=mesh['dp'=16,'expert'=32] {'expert'}, dimensions={0}, use_global_device_ids=true | all-gather | bytes 135168 | tf_op jit(solution)/shard_map/all_gather | solution.py:63
  58.2 0.3 reduce_window_sum.13
  58.7 15.5 %scatter_custom_fusion = f32[1280]{0:T(1024)S(1)} fusion(s32[4096]{0:T(1024)S(1)} %bitcast.45, f32[4096]{0:T(1024)S(1)} %get-tuple-element.10, f32[]{:T(128)} %constant.8.clone.1), kind=kCustom, calls=%fused_computation.56 | custom fusion | bytes 5124 | tf_op jit(solution)/shard_map/scatter | solution.py:74
  74.2 18.3 %scatter_custom_fusion.1 = bf16[1280,256]{1,0:T(8,128)(2,1)S(1)} fusion(s32[4096]{0:T(1024)S(1)} %bitcast.46, bf16[4096,256]{1,0:T(8,128)(2,1)} %all-gather.3.cloned.1.call-done, bf16[]{:T(256)} %constant.13.clone.1), kind=kCustom, calls=%fused_computation.46 | custom fusion | bytes 655872 | tf_op jit(solution)/shard_map/scatter | solution.py:72
  92.5 3.2 convolution_convert_fusion.1
  95.7 2.0 convolution_convert_fusion.2
  97.7 38.0 %all-gather.5.cloned.1.call-done = bf16[4096,256]{1,0:T(8,128)(2,1)} async-done(((bf16[128,256]{1,0:T(8,128)(2,1)}), bf16[4096,256]{1,0:T(8,128)(2,1)}) %all-gather.5.cloned.1.call-update) | async-done | bytes 2097168 | tf_op jit(solution)/shard_map/all_gather | solution.py:60
  135.7 18.3 %scatter_custom_fusion.2 = bf16[1280,256]{1,0:T(8,128)(2,1)S(1)} fusion(s32[4096]{0:T(1024)S(1)} %bitcast.47, bf16[4096,256]{1,0:T(8,128)(2,1)} %all-gather.5.cloned.1.call-done, bf16[]{:T(256)} %constant.13.clone.1), kind=kCustom, calls=%fused_computation.44 | custom fusion | bytes 655872 | tf_op jit(solution)/shard_map/scatter | solution.py:90
  154.0 2.0 convolution_convert_fusion
  156.1 0.2 reduce-scatter.5.cloned.1.call-start
  156.3 167.8 %all-reduce.3.cloned.1.call-done = (bf16[1280,768]{1,0:T(8,128)(2,1)}, bf16[1280,768]{1,0:T(8,128)(2,1)}, bf16[1280,768]{1,0:T(8,128)(2,1)}) async-done(((bf16[1280,768]{1,0:T(8,128)(2,1)}, bf16[1280,768]{1,0:T(8,128)(2,1)}, bf16[1280,768]{1,0:T(8,128)(2,1)}), (bf16[1280,768]{1,0:T(8,128)(2,1)}, bf16[1280,768]{1,0:T(8,128)(2,1)}, bf16[1280,768]{1,0:T(8,128)(2,1)})) %all-reduce.3.cloned.1.call-update) | async-done | bytes 5898256 | tf_op jit(solution)/shard_map/psum | solution.py:24
  324.2 4.2 fusion.4
  328.4 0.7 fusion.12
  329.2 0.7 fusion.19
  329.9 0.4 copy-done.7
  330.3 0.6 copy-done.3
  330.9 0.7 fusion.14
  331.7 16.1 %gather_fusion.1 = f32[4096,256]{1,0:T(8,128)} fusion(f32[1280,256]{1,0:T(8,128)S(1)} %fusion.14, s32[4096]{0:T(1024)S(1)} %broadcast_clamp_fusion), kind=kCustom, calls=%fused_computation.1 | custom fusion | bytes 8404992 | tf_op jit(solution)/shard_map/gather | solution.py:97
  347.8 16.2 %gather_fusion = f32[4096,256]{1,0:T(8,128)} fusion(f32[1280,256]{1,0:T(8,128)S(1)} %fusion.12, s32[4096]{0:T(1024)S(1)} %broadcast_clamp_fusion), kind=kCustom, calls=%fused_computation | custom fusion | bytes 8404992 | tf_op jit(solution)/shard_map/gather | solution.py:84
  364.0 5.1 multiply_convert_fusion
  369.2 0.5 reduce-scatter.3.cloned.1.call-update
  369.7 0.9 copy-done.4
  370.7 0.1 copy-done.6
  370.8 1.6 convolution_bitcast_fusion.1
  372.4 1.6 convolution_bitcast_fusion.2
  374.0 0.2 copy-done.10
  374.2 1.8 convolution_bitcast_fusion
  376.0 91.4 %reduce-scatter.5.cloned.1.call-done = bf16[128,256]{1,0:T(8,128)(2,1)} async-done(((bf16[4096,256]{1,0:T(8,128)(2,1)}), bf16[128,256]{1,0:T(8,128)(2,1)}) %reduce-scatter.5.cloned.1.call-update) | async-done | bytes 65552 | tf_op jit(solution)/shard_map/reduce_scatter | solution.py:96
  467.5 106.4 %reduce-scatter.3.cloned.1.call-done = bf16[128,256]{1,0:T(8,128)(2,1)} async-done(((bf16[4096,256]{1,0:T(8,128)(2,1)}), bf16[128,256]{1,0:T(8,128)(2,1)}) %reduce-scatter.3.cloned.1.call-update) | async-done | bytes 65552 | tf_op jit(solution)/shard_map/reduce_scatter | solution.py:83
  (36 shorter events, 0.5 us)
Async XLA Ops:
  7.2 146.9 %copy-start = (bf16[1,768,256]{2,1,0:T(8,128)(2,1)S(1)}, bf16[1,768,256]{2,1,0:T(8,128)(2,1)}, u32[]{:S(2)}) copy-start(bf16[1,768,256]{2,1,0:T(8,128)(2,1)} %param.12) | copy-start | bytes 1179652
  7.2 67.0 %all-gather.3.cloned.1.call-start = ((), (), s32[]{:S(2)}) async-start(), calls=%async_computation.2 | async-start | bytes 2162688 | tf_op jit(solution)/shard_map/all_gather | solution.py:59
  7.9 127.8 %all-gather.5.cloned.1.call-start = ((), (), s32[]{:S(2)}) async-start(), calls=%async_computation.4 | async-start | bytes 2162688 | tf_op jit(solution)/shard_map/all_gather | solution.py:60
  8.7 315.5 %all-reduce.3.cloned.1.call-start = ((), (), s32[]{:S(2)}) async-start(), calls=%async_computation.6 | async-start | bytes 11796480 | tf_op jit(solution)/shard_map/psum | solution.py:24
  58.2 37.6 %copy-start.11 = (bf16[1,256,768]{2,1,0:T(8,128)(2,1)S(1)}, bf16[1,256,768]{2,1,0:T(8,128)(2,1)}, u32[]{:S(2)}) copy-start(bf16[1,256,768]{2,1,0:T(8,128)(2,1)} %param.10) | copy-start | bytes 1179652
  92.5 5.2 copy-start.5
  154.0 2.0 copy-start.9
  156.1 311.4 %reduce-scatter.5.cloned.1.call-start = ((), (), s32[]{:S(2)}) async-start(), calls=%async_computation.5 | async-start | bytes 2162688 | tf_op jit(solution)/shard_map/reduce_scatter | solution.py:96
  328.4 1.5 copy-start.1
  328.4 1.9 copy-start.7
  328.4 2.5 copy-start.3
  329.1 1.8 copy-start.12
  369.1 1.5 copy-start.4
  369.1 1.7 copy-start.6
  369.1 204.7 %reduce-scatter.3.cloned.1.call-start = ((), (), s32[]{:S(2)}) async-start(), calls=%async_computation.3 | async-start | bytes 2162688 | tf_op jit(solution)/shard_map/reduce_scatter | solution.py:83
  370.8 1.6 copy-start.2
  372.4 1.6 copy-start.8
  372.4 1.8 copy-start.10
Sparse Core Ops, SparseCore 0:
  11.1 62.9 all-gather.2
  77.3 58.3 all-gather.4
  156.2 167.9 all-reduce.2
  369.3 98.1 reduce-scatter.4
  472.3 101.5 reduce-scatter.2
where the time goes:
time: 581 us; the launch traced here: 580 us
  waiting for transfers between devices  406 us (70%)
  local copies, waits for them, and re-layouts  86.8 us (15%)
  blocking collectives  49.4 us (9%)
  matrix products  14.3 us (2%)
  between operations  14 us (2%)
  other arithmetic  9.82 us (2%)
    psum x1, waiting for transfers between devices, expert_forward(): lax.psum(partial_up.astype(jnp.bfloat16), 'dp').astype(jnp.float32)  168 us
    reduce_scatter x1, waiting for transfers between devices, shards(): lax.psum_scatter((weighted[safe_row] * present).astype(jnp.bfloat16), 'ex...  106 us
    reduce_scatter x1, waiting for transfers between devices, shards(): lax.psum_scatter((back_rows.astype(jnp.float32)[safe_row] * present).asty...  91.4 us
    all_gather x1, waiting for transfers between devices, shards(): lax.all_gather(out_grad, 'expert', axis=0, tiled=True)  38 us
    scatter x2, local copies, waits for them, and re-layouts, shards(): jnp.zeros((row_total, width), jnp.bfloat16).at[dest_row]  36.6 us
    all_gather x1, blocking collectives, shards(): lax.all_gather(route_weights, 'expert', axis=0, tiled=True)  27.1 us
    all_gather x1, blocking collectives, shards(): every_ids = lax.all_gather(route_ids, 'expert', axis=0, tiled=True)  22.3 us
    gather x1, local copies, waits for them, and re-layouts, shards(): weighted[safe_row] * present  16.2 us
  transfers between devices with their start and end apart: 5, of which 4 were waited for; matrix products, arithmetic and copies ran while one was open for 8% of the time, Pallas kernels for 0%

commit v1 on v0

--- a/solution.py
+++ b/solution.py
@@ -21,7 +21,7 @@
     partial_up = jnp.dot(expert_rows, weight_u, preferred_element_type=jnp.float32)
     gate_pre, up_pre = (
         lax.psum(partial_gate.astype(jnp.bfloat16), "dp").astype(jnp.float32),
-        lax.psum(partial_up.astype(jnp.bfloat16), "dp").astype(jnp.float32),
+        jnp.sum(lax.all_gather(partial_up.astype(jnp.bfloat16), "dp"), axis=0).astype(jnp.float32),
     )
     hidden = (jax.nn.silu(gate_pre) * up_pre).astype(jnp.bfloat16)
     produced = jnp.dot(hidden, weight_d, preferred_element_type=jnp.float32).astype(jnp.bfloat16)

time: 581 us -> 887 us (1.53)
  waiting for transfers between devices: 406 us -> 701 us
  other arithmetic: 9.82 us -> 20.9 us
    all_gather x0 -> x1, waiting for transfers between devices: none -> 317 us  [expert_forward(): lax.all_gather(partial_up.astype(jnp.bfloat16), 'dp')]
    psum x1, waiting for transfers between devices: 168 us -> 145 us  [expert_forward(): lax.psum(partial_gate.astype(jnp.bfloat16), 'dp').astype(jnp.float32)]
    all_gather x1, waiting for transfers between devices: 0.02 us -> 15.5 us  [shards(): lax.all_gather(tokens, 'expert', axis=0, tiled=True)]
    all_gather x1, waiting for transfers between devices: 38 us -> 24.3 us  [shards(): lax.all_gather(out_grad, 'expert', axis=0, tiled=True)]
    reduce_sum x0 -> x1, other arithmetic: none -> 11.3 us  [expert_forward(): jnp.sum(lax.all_gather(partial_up.astype(jnp.bfloat16), 'dp'), axis=0)]
  transfers between devices with their start and end apart: 5 -> 6, of which waited for: 4 -> 6; matrix products, arithmetic and copies ran while one was open for 8% -> 9% of each run, Pallas kernels for 0% -> 0%
where the time goes in v1:
time: 887 us
  waiting for transfers between devices  701 us (79%)
  local copies, waits for them, and re-layouts  86.7 us (10%)
  blocking collectives  49.4 us (6%)
  other arithmetic  20.9 us (2%)
  matrix products  14.3 us (2%)
  between operations  14.3 us (2%)
    all_gather x1, waiting for transfers between devices, expert_forward(): lax.all_gather(partial_up.astype(jnp.bfloat16), 'dp')  317 us
    psum x1, waiting for transfers between devices, expert_forward(): lax.psum(partial_gate.astype(jnp.bfloat16), 'dp').astype(jnp.float32)  145 us
    reduce_scatter x1, waiting for transfers between devices, shards(): lax.psum_scatter((weighted[safe_row] * present).astype(jnp.bfloat16), 'ex...  106 us
    reduce_scatter x1, waiting for transfers between devices, shards(): lax.psum_scatter((back_rows.astype(jnp.float32)[safe_row] * present).asty...  90.8 us
    scatter x2, local copies, waits for them, and re-layouts, shards(): jnp.zeros((row_total, width), jnp.bfloat16).at[dest_row]  36.6 us
    all_gather x1, blocking collectives, shards(): lax.all_gather(route_weights, 'expert', axis=0, tiled=True)  27.1 us
    all_gather x1, waiting for transfers between devices, shards(): lax.all_gather(out_grad, 'expert', axis=0, tiled=True)  24.3 us
    all_gather x1, blocking collectives, shards(): every_ids = lax.all_gather(route_ids, 'expert', axis=0, tiled=True)  22.3 us
  transfers between devices with their start and end apart: 6, of which 6 were waited for; matrix products, arithmetic and copies ran while one was open for 9% of the time, Pallas kernels for 0%

profile of v1, /device:TPU:2, one launch (start us, length us, event | category | flops | bytes accessed | tf_op | source)
XLA Modules:
  0.0 886.7 jit_solution(1524954169812980217)
XLA Ops:
  7.2 0.7 all-gather.5.cloned.1.call-update
  8.0 0.7 all-gather.7.cloned.1.call-update
  8.7 27.1 %all_gather.19 = bf16[4096,8]{0,1:T(8,128)(2,1)S(1)} all-gather(bf16[128,8]{0,1:T(8,128)(2,1)} %param.9), channel_id=1, replica_groups=mesh['dp'=16,'expert'=32] {'expert'}, dimensions={0}, use_global_device_ids=true | all-gather | bytes 67584 | tf_op jit(solution)/shard_map/all_gather | solution.py:61
  35.8 22.3 %all_gather.18 = s32[4096,8]{0,1:T(8,128)S(1)} all-gather(s32[128,8]{0,1:T(8,128)} %param.8), channel_id=1, replica_groups=mesh['dp'=16,'expert'=32] {'expert'}, dimensions={0}, use_global_device_ids=true | all-gather | bytes 135168 | tf_op jit(solution)/shard_map/all_gather | solution.py:63
  58.2 0.3 reduce_window_sum.13
  58.6 15.5 %all-gather.5.cloned.1.call-done = bf16[4096,256]{1,0:T(8,128)(2,1)} async-done(((bf16[128,256]{1,0:T(8,128)(2,1)}), bf16[4096,256]{1,0:T(8,128)(2,1)}) %all-gather.5.cloned.1.call-update) | async-done | bytes 2097168 | tf_op jit(solution)/shard_map/all_gather | solution.py:59
  74.2 18.3 %scatter_custom_fusion.1 = bf16[1280,256]{1,0:T(8,128)(2,1)S(1)} fusion(s32[4096]{0:T(1024)S(1)} %bitcast.47, bf16[4096,256]{1,0:T(8,128)(2,1)} %all-gather.5.cloned.1.call-done, bf16[]{:T(256)} %constant.13.clone.1), kind=kCustom, calls=%fused_computation.46 | custom fusion | bytes 655872 | tf_op jit(solution)/shard_map/scatter | solution.py:72
  92.5 3.2 convolution_convert_fusion.1
  95.7 15.5 %scatter_custom_fusion = f32[1280]{0:T(1024)S(1)} fusion(s32[4096]{0:T(1024)S(1)} %bitcast.48, f32[4096]{0:T(1024)S(1)} %get-tuple-element.9, f32[]{:T(128)} %constant.8.clone.1), kind=kCustom, calls=%fused_computation.56 | custom fusion | bytes 5124 | tf_op jit(solution)/shard_map/scatter | solution.py:74
  111.3 24.3 %all-gather.7.cloned.1.call-done = bf16[4096,256]{1,0:T(8,128)(2,1)} async-done(((bf16[128,256]{1,0:T(8,128)(2,1)}), bf16[4096,256]{1,0:T(8,128)(2,1)}) %all-gather.7.cloned.1.call-update) | async-done | bytes 2097168 | tf_op jit(solution)/shard_map/all_gather | solution.py:60
  135.6 18.3 %scatter_custom_fusion.2 = bf16[1280,256]{1,0:T(8,128)(2,1)S(1)} fusion(s32[4096]{0:T(1024)S(1)} %bitcast.49, bf16[4096,256]{1,0:T(8,128)(2,1)} %all-gather.7.cloned.1.call-done, bf16[]{:T(256)} %constant.13.clone.1), kind=kCustom, calls=%fused_computation.44 | custom fusion | bytes 655872 | tf_op jit(solution)/shard_map/scatter | solution.py:90
  153.9 1.9 convolution_convert_fusion.2
  155.8 2.0 convolution_convert_fusion
  158.1 316.9 %all-gather.9.cloned.1.call-done = bf16[20480,768]{1,0:T(8,128)(2,1)} async-done(((bf16[1280,768]{1,0:T(8,128)(2,1)}), bf16[20480,768]{1,0:T(8,128)(2,1)}) %all-gather.9.cloned.1.call-update) | async-done | bytes 31457296 | tf_op jit(solution)/shard_map/all_gather | solution.py:24
  475.1 11.3 %reduce_sum.35 = bf16[1280,768]{1,0:T(8,128)(2,1)S(1)} reduce(bf16[16,1280,768]{2,1,0:T(8,128)(2,1)} %bitcast.41, bf16[]{:T(256)} %constant.13.clone.1), dimensions={0}, to_apply=%region_6.7 | reduce | flops 14745600 | bytes 33423362 | tf_op jit(solution)/shard_map/reduce_sum | solution.py:24
  486.3 144.7 %all-reduce.3.cloned.1.call-done = (bf16[1280,768]{1,0:T(8,128)(2,1)}, bf16[1280,768]{1,0:T(8,128)(2,1)}) async-done(((bf16[1280,768]{1,0:T(8,128)(2,1)}, bf16[1280,768]{1,0:T(8,128)(2,1)}), (bf16[1280,768]{1,0:T(8,128)(2,1)}, bf16[1280,768]{1,0:T(8,128)(2,1)})) %all-reduce.3.cloned.1.call-update) | async-done | bytes 3932176 | tf_op jit(solution)/shard_map/psum | solution.py:23
  631.1 3.9 fusion.4
  635.1 0.7 fusion.12
  635.8 0.7 fusion.19
  636.5 0.4 copy-done.8
  636.9 0.7 copy-done.4
  637.7 0.7 fusion.14
  638.4 16.1 %gather_fusion.1 = f32[4096,256]{1,0:T(8,128)} fusion(f32[1280,256]{1,0:T(8,128)S(1)} %fusion.14, s32[4096]{0:T(1024)S(1)} %broadcast_clamp_fusion), kind=kCustom, calls=%fused_computation.1 | custom fusion | bytes 8404992 | tf_op jit(solution)/shard_map/gather | solution.py:97
  654.5 16.0 %gather_fusion = f32[4096,256]{1,0:T(8,128)} fusion(f32[1280,256]{1,0:T(8,128)S(1)} %fusion.12, s32[4096]{0:T(1024)S(1)} %broadcast_clamp_fusion), kind=kCustom, calls=%fused_computation | custom fusion | bytes 8404992 | tf_op jit(solution)/shard_map/gather | solution.py:84
  670.5 5.2 multiply_convert_fusion
  675.8 0.5 reduce-scatter.3.cloned.1.call-update
  676.4 0.9 copy-done.5
  677.4 1.6 convolution_bitcast_fusion.1
  679.0 1.6 convolution_bitcast_fusion.2
  680.8 1.8 convolution_bitcast_fusion
  682.6 90.8 %reduce-scatter.5.cloned.1.call-done = bf16[128,256]{1,0:T(8,128)(2,1)} async-done(((bf16[4096,256]{1,0:T(8,128)(2,1)}), bf16[128,256]{1,0:T(8,128)(2,1)}) %reduce-scatter.5.cloned.1.call-update) | async-done | bytes 65552 | tf_op jit(solution)/shard_map/reduce_scatter | solution.py:96
  773.5 106.4 %reduce-scatter.3.cloned.1.call-done = bf16[128,256]{1,0:T(8,128)(2,1)} async-done(((bf16[4096,256]{1,0:T(8,128)(2,1)}), bf16[128,256]{1,0:T(8,128)(2,1)}) %reduce-scatter.3.cloned.1.call-update) | async-done | bytes 65552 | tf_op jit(solution)/shard_map/reduce_scatter | solution.py:83
  (42 shorter events, 1.1 us)
Async XLA Ops:
  7.2 148.7 %copy-start = (bf16[1,768,256]{2,1,0:T(8,128)(2,1)S(1)}, bf16[1,768,256]{2,1,0:T(8,128)(2,1)}, u32[]{:S(2)}) copy-start(bf16[1,768,256]{2,1,0:T(8,128)(2,1)} %param.12) | copy-start | bytes 1179652
  7.2 67.0 %all-gather.5.cloned.1.call-start = ((), (), s32[]{:S(2)}) async-start(), calls=%async_computation.2 | async-start | bytes 2162688 | tf_op jit(solution)/shard_map/all_gather | solution.py:59
  7.9 127.6 %all-gather.7.cloned.1.call-start = ((), (), s32[]{:S(2)}) async-start(), calls=%async_computation.4 | async-start | bytes 2162688 | tf_op jit(solution)/shard_map/all_gather | solution.py:60
  8.7 466.4 %all-gather.9.cloned.1.call-start = ((), (), s32[]{:S(2)}) async-start(), calls=%async_computation.6 | async-start | bytes 33423360 | tf_op jit(solution)/shard_map/all_gather | solution.py:24
  92.4 61.4 %copy-start.6 = (bf16[1280,256]{1,0:T(8,128)(2,1)}, bf16[1280,256]{1,0:T(8,128)(2,1)S(1)}, u32[]{:S(2)}) copy-start(bf16[1280,256]{1,0:T(8,128)(2,1)S(1)} %scatter_custom_fusion.1) | copy-start | bytes 1966084
  95.7 58.2 %copy-start.12 = (bf16[1,256,768]{2,1,0:T(8,128)(2,1)S(1)}, bf16[1,256,768]{2,1,0:T(8,128)(2,1)}, u32[]{:S(2)}) copy-start(bf16[1,256,768]{2,1,0:T(8,128)(2,1)} %param.10) | copy-start | bytes 1179652
  95.7 535.4 %all-reduce.3.cloned.1.call-start = ((), (), s32[]{:S(2)}) async-start(), calls=%async_computation.7 | async-start | bytes 7864320 | tf_op jit(solution)/shard_map/psum | solution.py:23
  153.9 4.0 copy-start.10
  157.9 615.6 %reduce-scatter.5.cloned.1.call-start = ((), (), s32[]{:S(2)}) async-start(), calls=%async_computation.5 | async-start | bytes 2162688 | tf_op jit(solution)/shard_map/reduce_scatter | solution.py:96
  635.0 1.5 copy-start.2
  635.0 1.9 copy-start.8
  635.0 2.6 copy-start.4
  635.8 1.9 copy-start.13
  675.8 1.5 copy-start.5
  675.8 1.7 copy-start.7
  675.8 204.1 %reduce-scatter.3.cloned.1.call-start = ((), (), s32[]{:S(2)}) async-start(), calls=%async_computation.3 | async-start | bytes 2162688 | tf_op jit(solution)/shard_map/reduce_scatter | solution.py:83
  677.4 1.6 copy-start.3
  679.0 1.6 copy-start.9
  679.0 1.8 copy-start.11
  679.0 200.8 %copy-start.1 = (bf16[1,768,256]{2,1,0:T(8,128)(2,1)S(1)}, bf16[1,768,256]{2,1,0:T(8,128)(2,1)}, u32[]{:S(2)}) copy-start(bf16[1,768,256]{2,1,0:T(8,128)(2,1)} %param.12) | copy-start | bytes 1179652
Sparse Core Ops, SparseCore 0:
  11.1 62.9 all-gather.4
  77.3 58.2 all-gather.6
  137.6 337.3 all-gather.8
  477.3 153.6 all-reduce.2
  675.9 97.5 reduce-scatter.4
  778.3 101.5 reduce-scatter.2
